TPU v7x, 32 devices: a whole 2x2x4 slice. The times are simulated.
32 devices in a mesh: dp: 8 (over z, y), row: 2 (over core), col: 2 (over x).
Axes of the slice: x: 2, y: 2, z: 4, core: 2. Of those that a mesh axis runs over, the one named last changes fastest.
Arguments:
- hidden_in: bfloat16 [4096, 960], P(('dp', 'col'), 'row')
- segment_ids: int32 [4096], P('dp'), may hold values from 0 to 4095, as said below
- position_ids: int32 [4096], P('dp'), may hold values from 0 to 2048, as said below
- attn_gain: float32 [960], P('row'), may hold values from 0.5 to 1.5
- query_weight: bfloat16 [960, 960], P('row', 'col')
- key_weight: bfloat16 [960, 320], P('row', 'col')
- value_matrix: bfloat16 [960, 320], P('row', 'col'), may hold values from -0.1875 to 0.1875
- output_weight: bfloat16 [960, 960], P('col', 'row'), may hold values from -0.75 to 0.75
- ffn_gain: float32 [960], P('row'), may hold values from 0.5 to 1.5
- gate_weight: bfloat16 [960, 2560], P('row', 'col'), may hold values from -0.1875 to 0.1875
- up_weight: bfloat16 [960, 2560], P('row', 'col'), may hold values from -0.1875 to 0.1875
- down_weight: bfloat16 [2560, 960], P('col', 'row'), may hold values from -0.125 to 0.125
- out_grad: bfloat16 [4096, 960], P(('dp', 'col'), 'row')
Outputs:
- hidden_out: bfloat16 [4096, 960], P(('dp', 'col'), 'row')
- hidden_in_grad: float32 [4096, 960], P(('dp', 'col'), 'row')
- attn_gain_grad: float32 [960], P('row')
- query_weight_grad: float32 [960, 960], P('row', 'col')
- key_weight_grad: float32 [960, 320], P('row', 'col')
- value_weight_grad: float32 [960, 320], P('row', 'col')
- output_weight_grad: float32 [960, 960], P('col', 'row')
- ffn_gain_grad: float32 [960], P('row')
- gate_weight_grad: float32 [2, 960, 1280], P('col', 'row', 'dp')
- up_weight_grad: float32 [2, 960, 1280], P('col', 'row', 'dp')
- down_weight_grad: float32 [2, 1280, 960], P('col', 'dp', 'row')
Inputs may be any that keep to these rules, and one draw needn't show every extreme that they name: `segment_ids`: segment numbers never fall from one token to the next, and the first token of each sequence of 512 tokens begins a new number. `position_ids`: within a document each token's position is one or two more than the previous token's; the first token of each sequence of 512 tokens has position 0.
All inputs are finite; a program needn't handle non-finite values.
Results may differ from a plain program's by a relative error of at most 0.02.
The roundings to bfloat16 on the way count: a program that leaves them out, or rounds other values in their place, can miss the bound.
Values may be sent and summed in bfloat16 or wider, within the bound.
A program may use at most 128 MiB of HBM per device.

v0:
```python
import jax
import jax.numpy as jnp
from jax import lax
from jax.sharding import PartitionSpec as P

MODEL_WIDTH = 960
QUERY_HEADS = 15
KEY_VALUE_HEADS = 5
HEAD_SIZE = 64


epsilon = 1e-05
rope_base = 10000.0
masked_score = -1e30


def rope_tables(position_row):
    half_size = HEAD_SIZE // 2
    frequency = rope_base ** (-(jnp.arange(half_size, dtype=jnp.float32) * 2.0) / HEAD_SIZE)
    angles = position_row.astype(jnp.float32)[:, None] * frequency[None, :]
    return (jnp.cos(angles), jnp.sin(angles))


def apply_rotary(values, cosine_table, sine_lookup, direction):
    half_size = values.shape[-1] // 2
    front_half = values[..., :half_size]
    back_half = values[..., half_size:]
    cosine_wide = cosine_table[:, None, :]
    sine_wide = direction * sine_lookup[:, None, :]
    return jnp.concatenate(
        [
            front_half * cosine_wide - back_half * sine_wide,
            back_half * cosine_wide + front_half * sine_wide,
        ],
        axis=-1,
    )


def matmul(left, right):
    return jnp.dot(left, right, preferred_element_type=jnp.float32)


def contract_rows(left, right):
    return lax.dot_general(
        left, right, (((0,), (0,)), ((), ())), preferred_element_type=jnp.float32
    )


def row_sums(values):
    return lax.psum(values, "row")


def gather_over_cols(values):
    return lax.all_gather(values, "col", axis=0, tiled=True)


def gather_over_rows(values):
    return lax.all_gather(values, "row", axis=0, tiled=True)


def sum_over_rows(partial_value):
    return lax.psum_scatter(partial_value, "row", scatter_dimension=0, tiled=True)


def sum_over_cols(partial_value):
    return lax.psum_scatter(partial_value, "col", scatter_dimension=0, tiled=True)


def to_heads(values):
    return lax.all_to_all(values, "col", split_axis=0, concat_axis=1, tiled=True)


def from_heads(values):
    return lax.all_to_all(values, "col", split_axis=1, concat_axis=0, tiled=True)


def norm_forward(residual, gain):
    mean_square = row_sums(jnp.sum(residual * residual, axis=1)) / MODEL_WIDTH
    inverse_rms = lax.rsqrt(mean_square + epsilon)
    unit_rows = residual * inverse_rms[:, None]
    return (unit_rows, inverse_rms, (unit_rows * gain[None, :]).astype(jnp.bfloat16))


def norm_backward(grad_normed, unit_rows, inverse_rms, gain):
    weighted = grad_normed * gain[None, :]
    inner_mean = row_sums(jnp.sum(weighted * unit_rows, axis=1)) / MODEL_WIDTH
    grad_input = inverse_rms[:, None] * (weighted - unit_rows * inner_mean[:, None])
    return (grad_input, jnp.sum(grad_normed * unit_rows, axis=0))


def attention_scores(query_group, key_group, allowed):
    scores = jnp.einsum(
        "qkgd,skd->kgqs", query_group, key_group, preferred_element_type=jnp.float32
    ) * HEAD_SIZE ** (-0.5)
    return jnp.where(allowed[None, None], scores, masked_score)


def on_device(
    hidden_in,
    segment_ids,
    position_ids,
    attn_gain,
    query_weight,
    key_weight,
    value_matrix,
    output_weight,
    ffn_gain,
    gate_weight,
    up_weight,
    down_weight,
    out_grad,
):
    n_rows = lax.axis_size("row")
    n_cols = lax.axis_size("col")
    sequence_length = segment_ids.shape[0]
    portion_length = sequence_length // (n_rows * n_cols)
    part_start = (lax.axis_index("row") * n_cols + lax.axis_index("col")) * portion_length
    query_cols = query_weight.shape[1]
    kv_cols = key_weight.shape[1]
    block_cols = query_cols + 2 * kv_cols
    heads_per_group = QUERY_HEADS // KEY_VALUE_HEADS
    ffn_cols = gate_weight.shape[1]
    residual = hidden_in.astype(jnp.float32)
    unit_one, inverse_one, normed_one = norm_forward(residual, attn_gain)
    normed_one_all = gather_over_cols(normed_one)
    proj_weight = jnp.concatenate([query_weight, key_weight, value_matrix], axis=1)
    projected = sum_over_rows(matmul(normed_one_all, proj_weight)).astype(jnp.bfloat16)
    grouped = to_heads(projected).reshape(portion_length, n_cols, block_cols)
    query_part = grouped[:, :, :query_cols].reshape(portion_length, n_cols * query_cols)
    key_portion = grouped[:, :, query_cols : query_cols + kv_cols].reshape(
        portion_length, n_cols * kv_cols
    )
    value_part = grouped[:, :, query_cols + kv_cols :].reshape(portion_length, n_cols * kv_cols)
    cosine_table, sine_lookup = rope_tables(
        lax.dynamic_slice_in_dim(position_ids, part_start, portion_length)
    )
    query_rotated = apply_rotary(
        query_part.astype(jnp.float32).reshape(portion_length, QUERY_HEADS, HEAD_SIZE),
        cosine_table,
        sine_lookup,
        1.0,
    ).astype(jnp.bfloat16)
    key_rotated = apply_rotary(
        key_portion.astype(jnp.float32).reshape(portion_length, KEY_VALUE_HEADS, HEAD_SIZE),
        cosine_table,
        sine_lookup,
        1.0,
    ).astype(jnp.bfloat16)
    key_token_rows, value_token_rows = (
        lax.all_gather(
            key_rotated.reshape(portion_length, KEY_VALUE_HEADS * HEAD_SIZE),
            ("row", "col"),
            axis=0,
            tiled=True,
        ),
        lax.all_gather(value_part, ("row", "col"), axis=0, tiled=True),
    )
    part_segments = lax.dynamic_slice_in_dim(segment_ids, part_start, portion_length)
    query_index = part_start + jnp.arange(portion_length, dtype=jnp.int32)
    key_index = jnp.arange(sequence_length, dtype=jnp.int32)
    allowed = (part_segments[:, None] == segment_ids[None, :]) & (
        key_index[None, :] <= query_index[:, None]
    )
    query_group = query_rotated.reshape(portion_length, KEY_VALUE_HEADS, heads_per_group, HEAD_SIZE)
    key_group = key_token_rows.reshape(sequence_length, KEY_VALUE_HEADS, HEAD_SIZE)
    value_group = value_token_rows.reshape(sequence_length, KEY_VALUE_HEADS, HEAD_SIZE)
    scores = attention_scores(query_group, key_group, allowed)
    row_max = jnp.max(scores, axis=-1, keepdims=True)
    log_total = row_max + jnp.log(jnp.sum(jnp.exp(scores - row_max), axis=-1, keepdims=True))
    attn_probs = jnp.exp(scores - log_total).astype(jnp.bfloat16)
    attended_output = (
        jnp.einsum("kgqs,skd->qkgd", attn_probs, value_group, preferred_element_type=jnp.float32)
        .astype(jnp.bfloat16)
        .reshape(portion_length, QUERY_HEADS * HEAD_SIZE)
    )
    attended_rows = from_heads(attended_output)
    attended_all = gather_over_rows(attended_rows)
    mid = residual + sum_over_cols(matmul(attended_all, output_weight))
    unit_two, inverse_two, normed_two = norm_forward(mid, ffn_gain)
    normed_two_all = gather_over_cols(normed_two)
    ffn_weight = jnp.concatenate([gate_weight, up_weight], axis=1)
    ffn_pre = sum_over_rows(matmul(normed_two_all, ffn_weight))
    gate_pre = ffn_pre[:, :ffn_cols]
    up_pre = ffn_pre[:, ffn_cols:]
    gate_sigmoid = jax.nn.sigmoid(gate_pre)
    gate_silu = gate_pre * gate_sigmoid
    inner_act = (gate_silu * up_pre).astype(jnp.bfloat16)
    inner_all = gather_over_rows(inner_act)
    final = mid + sum_over_cols(matmul(inner_all, down_weight))
    hidden_out = final.astype(jnp.bfloat16)
    grad_all = gather_over_cols(out_grad)
    inner_back = gather_over_rows(inner_act)
    down_wgrad = contract_rows(inner_back, grad_all)
    inner_grad = sum_over_rows(matmul(grad_all, down_weight.T))
    silu_slope = gate_sigmoid * (1.0 + gate_pre * (1.0 - gate_sigmoid))
    both_grad = jnp.concatenate(
        [
            (inner_grad * up_pre * silu_slope).astype(jnp.bfloat16),
            (inner_grad * gate_silu).astype(jnp.bfloat16),
        ],
        axis=1,
    )
    both_all = gather_over_rows(both_grad)
    normed_two_back = gather_over_cols(normed_two)
    ffn_wgrad = contract_rows(normed_two_back, both_all)
    normed_two_grad = sum_over_cols(matmul(both_all, ffn_weight.T))
    mid_part, ffn_gain_part = norm_backward(normed_two_grad, unit_two, inverse_two, ffn_gain)
    mid_grad = out_grad.astype(jnp.float32) + mid_part
    mid_grad_all = gather_over_cols(mid_grad.astype(jnp.bfloat16))
    attended_back = gather_over_rows(attended_rows)
    out_wgrad = contract_rows(attended_back, mid_grad_all)
    attended_gradient = to_heads(
        sum_over_rows(matmul(mid_grad_all, output_weight.T)).astype(jnp.bfloat16)
    )
    gradient_group = attended_gradient.reshape(
        portion_length, KEY_VALUE_HEADS, heads_per_group, HEAD_SIZE
    )
    attended_group = attended_output.reshape(
        portion_length, KEY_VALUE_HEADS, heads_per_group, HEAD_SIZE
    )
    grad_dot = jnp.transpose(
        jnp.sum(gradient_group.astype(jnp.float32) * attended_group.astype(jnp.float32), axis=-1),
        (1, 2, 0),
    )
    scores_again = attention_scores(query_group, key_group, allowed)
    prob_exact = jnp.exp(scores_again - log_total)
    value_gradient = jnp.einsum(
        "kgqs,qkgd->skd",
        prob_exact.astype(jnp.bfloat16),
        gradient_group,
        preferred_element_type=jnp.float32,
    )
    prob_grad = jnp.einsum(
        "qkgd,skd->kgqs", gradient_group, value_group, preferred_element_type=jnp.float32
    )
    score_grad = (prob_exact * (prob_grad - grad_dot[..., None]) * HEAD_SIZE ** (-0.5)).astype(
        jnp.bfloat16
    )
    query_grad = jnp.einsum(
        "kgqs,skd->qkgd", score_grad, key_group, preferred_element_type=jnp.float32
    )
    key_gradient = jnp.einsum(
        "kgqs,qkgd->skd", score_grad, query_group, preferred_element_type=jnp.float32
    )
    key_gradient_total, value_total = (
        lax.psum_scatter(
            key_gradient.reshape(sequence_length, KEY_VALUE_HEADS * HEAD_SIZE),
            ("row", "col"),
            scatter_dimension=0,
            tiled=True,
        ),
        lax.psum_scatter(
            value_gradient.reshape(sequence_length, KEY_VALUE_HEADS * HEAD_SIZE),
            ("row", "col"),
            scatter_dimension=0,
            tiled=True,
        ),
    )
    query_back = apply_rotary(
        query_grad.reshape(portion_length, QUERY_HEADS, HEAD_SIZE), cosine_table, sine_lookup, -1.0
    ).astype(jnp.bfloat16)
    key_backward = apply_rotary(
        key_gradient_total.reshape(portion_length, KEY_VALUE_HEADS, HEAD_SIZE),
        cosine_table,
        sine_lookup,
        -1.0,
    ).astype(jnp.bfloat16)
    regrouped = jnp.concatenate(
        [
            query_back.reshape(portion_length, n_cols, query_cols),
            key_backward.reshape(portion_length, n_cols, kv_cols),
            value_total.astype(jnp.bfloat16).reshape(portion_length, n_cols, kv_cols),
        ],
        axis=2,
    ).reshape(portion_length, n_cols * block_cols)
    proj_grad = from_heads(regrouped)
    proj_all = gather_over_rows(proj_grad)
    normed_one_back = gather_over_cols(normed_one)
    proj_wgrad = contract_rows(normed_one_back, proj_all)
    normed_one_grad = sum_over_cols(matmul(proj_all, proj_weight.T))
    in_part, attn_gain_part = norm_backward(normed_one_grad, unit_one, inverse_one, attn_gain)
    hidden_in_grad = mid_grad + in_part
    query_wgrad = proj_wgrad[:, :query_cols]
    key_wgrad = proj_wgrad[:, query_cols : query_cols + kv_cols]
    value_wgrad = proj_wgrad[:, query_cols + kv_cols :]
    col_gains = lax.psum((attn_gain_part, ffn_gain_part), "col")
    joined = lax.psum(
        (query_wgrad, key_wgrad, value_wgrad, out_wgrad, col_gains[0], col_gains[1]), "dp"
    )
    attn_totals = (joined[0], joined[1], joined[2], joined[3])
    gain_totals = (joined[4], joined[5])
    mlp_totals = (
        lax.psum_scatter(ffn_wgrad[None, :, :ffn_cols], "dp", scatter_dimension=2, tiled=True),
        lax.psum_scatter(ffn_wgrad[None, :, ffn_cols:], "dp", scatter_dimension=2, tiled=True),
        lax.psum_scatter(down_wgrad[None], "dp", scatter_dimension=1, tiled=True),
    )
    return (
        hidden_out,
        hidden_in_grad,
        gain_totals[0],
        attn_totals[0],
        attn_totals[1],
        attn_totals[2],
        attn_totals[3],
        gain_totals[1],
        mlp_totals[0],
        mlp_totals[1],
        mlp_totals[2],
    )


def solution(mesh):
    return jax.shard_map(
        on_device,
        mesh=mesh,
        in_specs=(
            P(("dp", "col"), "row"),
            P("dp"),
            P("dp"),
            P("row"),
            P("row", "col"),
            P("row", "col"),
            P("row", "col"),
            P("col", "row"),
            P("row"),
            P("row", "col"),
            P("row", "col"),
            P("col", "row"),
            P(("dp", "col"), "row"),
        ),
        out_specs=(
            P(("dp", "col"), "row"),
            P(("dp", "col"), "row"),
            P("row"),
            P("row", "col"),
            P("row", "col"),
            P("row", "col"),
            P("col", "row"),
            P("row"),
            P("col", "row", "dp"),
            P("col", "row", "dp"),
            P("col", "dp", "row"),
        ),
        check_vma=False,
    )
```

profile of v0, /device:TPU:0, one launch (start us, length us, event | category | flops | bytes accessed | tf_op | source)
XLA Modules:
  0.0 676.4 jit_solution(15995002472358062000)
XLA Ops:
  8.4 2.6 psum.84
  12.1 9.8 %all_gather.34 = bf16[512,480]{0,1:T(8,128)(2,1)S(1)} all-gather(bf16[256,480]{0,1:T(8,128)(2,1)S(1)} %fusion.10), channel_id=1, replica_groups=mesh['dp'=8,'row'=2,'col'=2] {'col'}, dimensions={0}, use_global_device_ids=true | all-gather | bytes 737280 | tf_op jit(solution)/shard_map/all_gather | solution.py:54
  21.8 1.2 copy.67
  23.1 1.1 copy.66
  24.2 3.2 fusion.18
  28.5 9.7 %reduce-scatter.11.cloned.1.call-done = f32[256,800]{0,1:T(8,128)} async-done(((f32[512,800]{0,1:T(8,128)}), f32[256,800]{0,1:T(8,128)}) %reduce-scatter.11.cloned.1.call-update) | async-done | bytes 819216 | tf_op jit(solution)/shard_map/reduce_scatter | solution.py:62
  38.2 1.9 copy_bitcast_fusion.1
  40.2 3.5 all-to-all-start
  43.8 7.3 %all-to-all-done = bf16[2,128,800]{1,2,0:T(8,128)(2,1)S(1)} async-done(((bf16[2,128,800]{1,2,0:T(8,128)(2,1)}), bf16[2,128,800]{1,2,0:T(8,128)(2,1)S(1)}, u32[]{:S(2)}, u32[]{:S(2)}) %all-to-all-start) | async-done | bytes 409632 | tf_op jit(solution)/shard_map/all_to_all | solution.py:70
  51.2 10.6 %all_gather.35 = bf16[512,320]{0,1:T(8,128)(2,1)S(1)} all-gather(bf16[128,320]{0,1:T(8,128)(2,1)S(1)} %bitcast.147), channel_id=1, replica_groups=mesh['dp'=8,'row'=2,'col'=2] {'row','col'}, dimensions={0}, use_global_device_ids=true | all-gather | bytes 409600 | tf_op jit(solution)/shard_map/all_gather | solution.py:156
  61.8 10.6 %all_gather.36 = bf16[512,320]{0,1:T(8,128)(2,1)S(1)} all-gather(bf16[128,320]{0,1:T(8,128)(2,1)S(1)} %bitcast.148), channel_id=1, replica_groups=mesh['dp'=8,'row'=2,'col'=2] {'row','col'}, dimensions={0}, use_global_device_ids=true | all-gather | bytes 409600 | tf_op jit(solution)/shard_map/all_gather | solution.py:150
  75.3 8.1 %all_to_all.67 = bf16[128,2,480]{0,2,1:T(8,128)(2,1)S(1)} all-to-all(bf16[128,2,480]{0,2,1:T(8,128)(2,1)S(1)} %bitcast.135), channel_id=1, replica_groups=mesh['dp'=8,'row'=2,'col'=2] {'col'}, dimensions={1} | all-to-all | bytes 491520 | tf_op jit(solution)/shard_map/all_to_all | solution.py:74
  83.4 2.2 all_gather.37
  85.6 1.4 fusion.36
  87.1 9.4 %all_gather.40 = bf16[512,480]{0,1:T(8,128)(2,1)S(1)} all-gather(bf16[256,480]{0,1:T(8,128)(2,1)S(1)} %copy-done.9), channel_id=1, replica_groups=mesh['dp'=8,'row'=2,'col'=2] {'col'}, dimensions={0}, use_global_device_ids=true | all-gather | bytes 737280 | tf_op jit(solution)/shard_map/all_gather | solution.py:54
  96.5 2.3 fusion.39
  98.9 2.5 constant_dynamic-update-slice_fusion.1
  101.4 2.5 constant_dynamic-update-slice_fusion
  103.9 3.6 reduce-scatter.13.cloned.1.call-done
  108.6 2.5 psum.85
  111.2 8.7 %all_gather.38 = bf16[512,480]{0,1:T(8,128)(2,1)S(1)} all-gather(bf16[256,480]{0,1:T(8,128)(2,1)S(1)} %multiply_convert_fusion.3), channel_id=1, replica_groups=mesh['dp'=8,'row'=2,'col'=2] {'col'}, dimensions={0}, use_global_device_ids=true | all-gather | bytes 737280 | tf_op jit(solution)/shard_map/all_gather | solution.py:54
  119.9 5.6 fusion.37
  125.6 13.3 %reduce-scatter.15.cloned.1.call-done = f32[256,2560]{1,0:T(8,128)} async-done(((f32[512,2560]{1,0:T(8,128)}), f32[256,2560]{1,0:T(8,128)}) %reduce-scatter.15.cloned.1.call-update) | async-done | bytes 2621456 | tf_op jit(solution)/shard_map/reduce_scatter | solution.py:62
  138.9 3.7 multiply_convert_fusion.1
  142.6 1.2 pad_maximum_fusion
  143.9 12.8 %all-gather.5.cloned.1.call-done = bf16[512,2560]{1,0:T(8,128)(2,1)} async-done(((bf16[256,2560]{1,0:T(8,128)(2,1)}), bf16[512,2560]{1,0:T(8,128)(2,1)}) %all-gather.5.cloned.1.call-update) | async-done | bytes 2621456 | tf_op jit(solution)/shard_map/all_gather | solution.py:58
  156.6 4.9 fusion.40
  161.6 21.0 %reduce-scatter.21.cloned.1.call-done = f32[256,480]{0,1:T(8,128)} async-done(((f32[512,480]{0,1:T(8,128)}), f32[256,480]{0,1:T(8,128)}) %reduce-scatter.21.cloned.1.call-update) | async-done | bytes 491536 | tf_op jit(solution)/shard_map/reduce_scatter | solution.py:66
  182.6 1.9 multiply_reduce_fusion
  184.4 2.4 psum.86
  186.9 1.2 fusion.33
  188.1 8.7 %all_gather.42 = bf16[512,480]{0,1:T(8,128)(2,1)S(1)} all-gather(bf16[256,480]{0,1:T(8,128)(2,1)S(1)} %fusion.33), channel_id=1, replica_groups=mesh['dp'=8,'row'=2,'col'=2] {'col'}, dimensions={0}, use_global_device_ids=true | all-gather | bytes 737280 | tf_op jit(solution)/shard_map/all_gather | solution.py:54
  196.8 1.4 fusion.45
  198.2 8.4 %reduce-scatter.23.cloned.1.call-done = f32[256,480]{0,1:T(8,128)} async-done(((f32[512,480]{0,1:T(8,128)}), f32[256,480]{0,1:T(8,128)}) %reduce-scatter.23.cloned.1.call-update) | async-done | bytes 491536 | tf_op jit(solution)/shard_map/reduce_scatter | solution.py:62
  207.7 8.3 %all_to_all.68 = bf16[2,128,480]{1,2,0:T(8,128)(2,1)S(1)} all-to-all(bf16[2,128,480]{1,2,0:T(8,128)(2,1)S(1)} %copy_bitcast_fusion.3), channel_id=1, replica_groups=mesh['dp'=8,'row'=2,'col'=2] {'col'}, dimensions={0} | all-to-all | bytes 491520 | tf_op jit(solution)/shard_map/all_to_all | solution.py:70
  216.0 4.1 fusion.22
  220.2 1.2 multiply_reduce_fusion.1
  221.3 3.8 fusion.2
  225.2 1.3 copy-done.2
  226.4 1.6 fusion.20
  228.7 2.1 fusion.41
  231.6 11.2 %reduce-scatter.27.cloned.1.call-done = f32[128,320]{0,1:T(8,128)} async-done(((f32[512,320]{0,1:T(8,128)}), f32[128,320]{0,1:T(8,128)}) %reduce-scatter.27.cloned.1.call-update) | async-done | bytes 163856 | tf_op jit(solution)/shard_map/reduce_scatter | solution.py:252
  242.8 1.6 convert_element_type.114
  244.3 23.4 %reduce-scatter.25.cloned.1.call-done = f32[128,320]{0,1:T(8,128)} async-done(((f32[512,320]{0,1:T(8,128)}), f32[128,320]{0,1:T(8,128)}) %reduce-scatter.25.cloned.1.call-update) | async-done | bytes 163856 | tf_op jit(solution)/shard_map/reduce_scatter | solution.py:246
  269.9 9.2 %all_to_all.69 = bf16[128,2,800]{0,2,1:T(8,128)(2,1)S(1)} all-to-all(bf16[128,2,800]{0,2,1:T(8,128)(2,1)S(1)} %pad_maximum_fusion.2), channel_id=1, replica_groups=mesh['dp'=8,'row'=2,'col'=2] {'col'}, dimensions={1} | all-to-all | bytes 819200 | tf_op jit(solution)/shard_map/all_to_all | solution.py:74
  279.1 2.4 all_gather.43
  282.4 1.6 fusion.17
  284.1 3.7 convolution_bitcast_fusion
  287.8 6.5 copy.78
  294.3 3.1 fusion.38
  297.5 3.2 fusion.44
  300.7 2.5 slice_bitcast_fusion
  303.2 6.4 copy.76
  309.7 6.5 copy.77
  316.2 1.4 fusion.43
  322.1 1.3 fusion.15
  323.4 4.9 all-reduce.5
  328.3 22.6 %all-reduce.3 = (f32[480]{0:T(512)}, f32[480]{0:T(512)}) all-reduce(f32[480]{0:T(512)S(1)} %get-tuple-element.68, f32[480]{0:T(512)S(1)} %get-tuple-element.69), channel_id=1, replica_groups=mesh['dp'=8,'row'=2,'col'=2] {'dp'}, use_global_device_ids=true, to_apply=%region_23.24 | all-reduce | flops 960 | bytes 7680 | tf_op jit(solution)/shard_map/psum | solution.py:287
  350.9 2.4 psum.87
  353.4 2.3 fusion.14
  355.7 304.2 %all-reduce.8.cloned.1.call-done = (f32[480,480]{0,1:T(8,128)}, f32[480,160]{0,1:T(8,128)}, f32[480,160]{0,1:T(8,128)}, f32[480,480]{1,0:T(8,128)}, f32[1,480,12...) async-done(((f32[480,480]{0,1:T(8,128)}, f32[480,160]{0,1:T(8,128)}, f32[480,160]{0,1:T(8,128)}, f32[480,480]{1,0:T(8,128)}, ...) | async-done | bytes 9830416 | tf_op jit(solution)/shard_map/psum | solution.py:287
  659.9 2.5 copy.79
  662.4 1.6 constant_dynamic-slice_fusion.1
  665.5 1.2 constant_dynamic-slice_fusion
  (144 shorter events, 22.2 us)
Async XLA Ops:
  7.2 89.3 %copy-start = (bf16[1280,480]{0,1:T(8,128)(2,1)S(1)}, bf16[1280,480]{0,1:T(8,128)(2,1)}, u32[]{:S(2)}) copy-start(bf16[1280,480]{0,1:T(8,128)(2,1)} %param.24) | copy-start | bytes 3686404
  7.2 31.0 %reduce-scatter.11.cloned.1.call-start = ((), (), s32[]{:S(2)}) async-start(), calls=%async_computation.14 | async-start | bytes 2457600 | tf_op jit(solution)/shard_map/reduce_scatter | solution.py:62
  21.8 5.7 copy-start.11
  23.1 4.4 copy-start.25
  24.2 3.3 copy-start.27
  24.2 3.3 copy-start.33
  40.2 11.0 %all-to-all-start = ((bf16[2,128,800]{1,2,0:T(8,128)(2,1)}), bf16[2,128,800]{1,2,0:T(8,128)(2,1)S(1)}, u32[]{:S(2)}, u32[]{:S(2)}) async-start(bf16[2,128,800]{1,2,0:T(8,128)(2,1)} %copy_bitcast_fusion.1), calls=%async_computation.1 | async-start | bytes 819200 | tf_op jit(solution)/shard_map/all_to_all | solution.py:70
  43.6 63.8 %reduce-scatter.13.cloned.1.call-start = ((), (), s32[]{:S(2)}) async-start(), calls=%async_computation.15 | async-start | bytes 1474560 | tf_op jit(solution)/shard_map/reduce_scatter | solution.py:66
  61.8 12.4 %copy-start.22 = (bf16[512,320]{0,1:T(8,128)(2,1)}, bf16[512,320]{0,1:T(8,128)(2,1)S(1)}, u32[]{:S(2)}) copy-start(bf16[512,320]{0,1:T(8,128)(2,1)S(1)} %all_gather.35) | copy-start | bytes 983044
  72.4 0.9 copy-start.8
  72.5 0.8 copy-start.17
  72.6 1.6 copy-start.15
  73.3 1.9 copy-start.1
  74.2 1.1 copy-start.31
  74.2 11.4 %copy-start.13 = (bf16[480,480]{1,0:T(8,128)(2,1)S(1)}, bf16[480,480]{1,0:T(8,128)(2,1)}, u32[]{:S(2)}) copy-start(bf16[480,480]{1,0:T(8,128)(2,1)} %param.20) | copy-start | bytes 1382404
  75.3 8.1 %copy-start.20 = (bf16[5,64,3,128]{3,1,2,0:T(8,128)(2,1)}, bf16[5,64,3,128]{3,1,2,0:T(8,128)(2,1)S(1)}, u32[]{:S(2)}) copy-start(bf16[5,64,3,128]{3,1,2,0:T(8,128)(2,1)S(1)} %convolution_convert_fusion) | copy-start | bytes 737284
  75.3 11.7 %copy-start.9 = (bf16[256,480]{0,1:T(8,128)(2,1)S(1)}, bf16[256,480]{0,1:T(8,128)(2,1)}, u32[]{:S(2)}) copy-start(bf16[256,480]{0,1:T(8,128)(2,1)} %param.25) | copy-start | bytes 737284
  87.0 38.6 %reduce-scatter.19.cloned.1.call-start = ((), (), s32[]{:S(2)}) async-start(), calls=%async_computation.19 | async-start | bytes 3932160 | tf_op jit(solution)/shard_map/reduce_scatter | solution.py:62
  96.5 2.3 copy-start.7
  98.9 8.6 %copy-start.3 = (bf16[256,480]{0,1:T(8,128)(2,1)S(1)}, bf16[256,480]{0,1:T(8,128)(2,1)}, u32[]{:S(2)}) copy-start(bf16[256,480]{0,1:T(8,128)(2,1)} %param.13) | copy-start | bytes 737284
  98.9 40.1 %reduce-scatter.15.cloned.1.call-start = ((), (), s32[]{:S(2)}) async-start(), calls=%async_computation.16 | async-start | bytes 7864320 | tf_op jit(solution)/shard_map/reduce_scatter | solution.py:62
  101.4 9.6 %copy-start.29 = (f32[480]{0:T(512)S(1)}, f32[480]{0:T(512)}, u32[]{:S(2)}) copy-start(f32[480]{0:T(512)} %param.21) | copy-start | bytes 5764
  125.5 31.1 %all-gather.5.cloned.1.call-start = ((), (), s32[]{:S(2)}) async-start(), calls=%async_computation.20 | async-start | bytes 3932160 | tf_op jit(solution)/shard_map/all_gather | solution.py:58
  143.8 38.7 %reduce-scatter.21.cloned.1.call-start = ((), (), s32[]{:S(2)}) async-start(), calls=%async_computation.21 | async-start | bytes 1474560 | tf_op jit(solution)/shard_map/reduce_scatter | solution.py:66
  161.5 45.1 %reduce-scatter.23.cloned.1.call-start = ((), (), s32[]{:S(2)}) async-start(), calls=%async_computation.22 | async-start | bytes 1474560 | tf_op jit(solution)/shard_map/reduce_scatter | solution.py:62
  186.8 10.0 %copy-start.14 = (bf16[480,480]{1,0:T(8,128)(2,1)S(1)}, bf16[480,480]{1,0:T(8,128)(2,1)}, u32[]{:S(2)}) copy-start(bf16[480,480]{1,0:T(8,128)(2,1)} %param.20) | copy-start | bytes 1382404
  198.2 44.6 %reduce-scatter.27.cloned.1.call-start = ((), (), s32[]{:S(2)}) async-start(), calls=%async_computation.24 | async-start | bytes 819200 | tf_op jit(solution)/shard_map/reduce_scatter | solution.py:252
  216.0 4.1 copy-start.21
  220.1 47.7 %reduce-scatter.25.cloned.1.call-start = ((), (), s32[]{:S(2)}) async-start(), calls=%async_computation.23 | async-start | bytes 819200 | tf_op jit(solution)/shard_map/reduce_scatter | solution.py:246
  221.3 5.1 copy-start.16
  221.3 5.1 copy-start.18
  225.1 1.3 copy-start.2
  228.1 56.1 %all-gather.3.cloned.1.call-start = ((), (), s32[]{:S(2)}) async-start(), calls=%async_computation.17 | async-start | bytes 1966080 | tf_op jit(solution)/shard_map/all_gather | solution.py:58
  228.6 93.4 %reduce-scatter.29.cloned.1.call-start = ((), (), s32[]{:S(2)}) async-start(), calls=%async_computation.25 | async-start | bytes 1474560 | tf_op jit(solution)/shard_map/reduce_scatter | solution.py:66
  267.8 14.6 %copy-start.26 = (bf16[480,160]{1,0:T(8,128)(2,1)S(1)}, bf16[480,160]{1,0:T(8,128)(2,1)}, u32[]{:S(2)}) copy-start(bf16[480,160]{1,0:T(8,128)(2,1)} %copy-done.25) | copy-start | bytes 460804
  267.8 14.6 %copy-start.28 = (bf16[480,160]{1,0:T(8,128)(2,1)S(1)}, bf16[480,160]{1,0:T(8,128)(2,1)}, u32[]{:S(2)}) copy-start(bf16[480,160]{1,0:T(8,128)(2,1)} %copy-done.27) | copy-start | bytes 460804
  267.8 14.6 %copy-start.34 = (bf16[480,480]{1,0:T(8,128)(2,1)S(1)}, bf16[480,480]{1,0:T(8,128)(2,1)}, u32[]{:S(2)}) copy-start(bf16[480,480]{1,0:T(8,128)(2,1)} %param.17) | copy-start | bytes 1382404
  281.5 0.9 copy-start.5
  284.1 69.3 %reduce-scatter.17.cloned.1.call-start = ((), (), s32[]{:S(2)}) async-start(), calls=%async_computation.18 | async-start | bytes 1474560 | tf_op jit(solution)/shard_map/reduce_scatter | solution.py:66
  297.4 362.4 %all-reduce.8.cloned.1.call-start = ((), (), s32[]{:S(2)}) async-start(), calls=%async_computation.26 | async-start | bytes 20971520 | tf_op jit(solution)/shard_map/psum | solution.py:287
  309.7 7.9 %copy-start.12 = (bf16[512,480]{0,1:T(8,128)(2,1)S(1)}, bf16[512,480]{0,1:T(8,128)(2,1)}, u32[]{:S(2)}) copy-start(bf16[512,480]{0,1:T(8,128)(2,1)} %copy-done.11) | copy-start | bytes 1474564
  316.2 1.4 copy-start.6
  320.2 0.7 copy-start.35
  320.2 1.9 copy-start.30
  320.2 3.2 copy-start.32
  320.2 33.2 %copy-start.4 = (f32[256,480]{0,1:T(8,128)S(1)}, f32[256,480]{0,1:T(8,128)}, u32[]{:S(2)}) copy-start(f32[256,480]{0,1:T(8,128)} %reduce-scatter.21.cloned.1.call-done) | copy-start | bytes 1474564
  320.2 33.2 %copy-start.10 = (bf16[256,480]{0,1:T(8,128)(2,1)S(1)}, bf16[256,480]{0,1:T(8,128)(2,1)}, u32[]{:S(2)}) copy-start(bf16[256,480]{0,1:T(8,128)(2,1)} %param.25) | copy-start | bytes 737284
  662.3 5.1 copy-start.24
  662.4 5.8 copy-start.23
  662.4 6.5 copy-start.19
Sparse Core Ops, SparseCore 0:
  27.6 10.5 reduce-scatter.10
  87.1 20.2 reduce-scatter.12
  109.7 10.6 reduce-scatter.18
  125.6 13.2 reduce-scatter.14
  143.9 12.6 all-gather.4
  161.7 20.8 reduce-scatter.20
  198.3 8.3 reduce-scatter.22
  220.2 22.5 reduce-scatter.26
  245.3 22.4 reduce-scatter.24
  269.7 9.4 all-gather.2
  284.2 19.6 reduce-scatter.28
  306.6 19.6 reduce-scatter.16
  332.3 327.4 all-reduce.7
where the time goes:
time: 678 us; the launch traced here: 676 us
  waiting for transfers between devices  416 us (61%)
  blocking collectives  125 us (18%)
  matrix products  45.8 us (7%)
  local copies, waits for them, and re-layouts  44.9 us (7%)
  other arithmetic  25.6 us (4%)
  between operations  15.1 us (2%)
    psum x1, waiting for transfers between devices, on_device(): lax.psum((query_wgrad, key_wgrad, value_wgrad, out_wgrad, col_gains[0], c...  304 us
    all_gather x4, blocking collectives, gather_over_cols(): return lax.all_gather(values, 'col', axis=0, tiled=True)  36.6 us
    reduce_scatter x4, waiting for transfers between devices, sum_over_rows(): lax.psum_scatter(partial_value, 'row', scatter_dimension=0, tiled=True)  31.5 us
    reduce_scatter x4, waiting for transfers between devices, sum_over_cols(): lax.psum_scatter(partial_value, 'col', scatter_dimension=0, tiled=True)  24.5 us
    dot_general x8, matrix products, matmul(): return jnp.dot(left, right, preferred_element_type=jnp.float32)  23.5 us
    reduce_scatter x1, waiting for transfers between devices, on_device(): lax.psum_scatter(key_gradient.reshape(sequence_length, KEY_VALUE_HEADS *...  23.4 us
    psum x1, blocking collectives, on_device(): lax.psum((query_wgrad, key_wgrad, value_wgrad, out_wgrad, col_gains[0], c...  22.6 us
    unnamed x85, local copies, waits for them, and re-layouts  18.3 us
  transfers between devices with their start and end apart: 14, of which 10 were waited for; matrix products, arithmetic and copies ran while one was open for 10% of the time, Pallas kernels for 0%

commit v1 on v0

v1 whole, which is shorter than its diff:
```python
import functools

import jax
import jax.numpy as jnp
from jax import lax
from jax.experimental import pallas as pl
from jax.experimental.pallas import tpu as pltpu
from jax.sharding import PartitionSpec as P

HEAD_SIZE = 64
QUERY_HEADS = 15
KEY_VALUE_HEADS = 5
epsilon = 1e-05
rope_base = 10000.0
masked_score = -1e30
MESH = pl.DeviceIdType.MESH
F32 = jnp.float32
BF16 = jnp.bfloat16
VM = pl.BlockSpec(memory_space=pltpu.VMEM)


def matmul(left, right):
    return jnp.dot(left, right, preferred_element_type=F32)


def contract_rows(left, right):
    return lax.dot_general(left, right, (((0,), (0,)), ((), ())), preferred_element_type=F32)


def contract_cols(left, right):
    return lax.dot_general(left, right, (((1,), (1,)), ((), ())), preferred_element_type=F32)


def greet(axes):
    barrier = pltpu.get_barrier_semaphore()
    for axis in axes:
        other = 1 - lax.axis_index(axis)
        pl.semaphore_signal(barrier, inc=1, device_id={axis: other}, device_id_type=MESH)
    pl.semaphore_wait(barrier, len(axes))


def remote(src, dst, send_sem, recv_sem, axis):
    return pltpu.make_async_remote_copy(
        src_ref=src,
        dst_ref=dst,
        send_sem=send_sem,
        recv_sem=recv_sem,
        device_id={axis: 1 - lax.axis_index(axis)},
        device_id_type=MESH,
    )


def call(body, outs, scratch, args, cid, vmem=60 * 2**20):
    return pl.pallas_call(
        body,
        out_shape=outs,
        in_specs=[VM] * len(args),
        out_specs=[VM] * len(outs),
        scratch_shapes=scratch,
        compiler_params=pltpu.CompilerParams(
            collective_id=cid, has_side_effects=cid is not None, vmem_limit_bytes=vmem
        ),
    )(*args)


def exchange(kinds, arrays, cid):
    n = len(arrays)

    def body(*refs):
        ins, outs, sems = refs[:n], refs[n : 2 * n], refs[2 * n]
        r, c = lax.axis_index("row"), lax.axis_index("col")
        greet(("row", "col") if "all" in kinds else ("row",))
        pending, firsts = [], []
        for i, kind in enumerate(kinds):
            if kind == "all":
                cp = remote(ins[i], outs[i].at[c, r], sems.at[i, 0], sems.at[i, 1], "col")
                cp.start()
                firsts.append((i, cp))
        for i, kind in enumerate(kinds):
            if kind == "all":
                src, keep, dst = ins[i], ins[i], outs[i].at[c, r]
            elif kind == "row":
                src, keep, dst = ins[i], ins[i], outs[i].at[r]
            elif kind == "lead":
                src, keep, dst = ins[i].at[1 - r], ins[i].at[r], outs[i].at[r]
            else:
                w = ins[i].shape[1] // 2
                src = ins[i].at[:, pl.ds(pl.multiple_of((1 - r) * w, 128), w)]
                keep = ins[i].at[:, pl.ds(pl.multiple_of(r * w, 128), w)]
                dst = outs[i].at[r]
            cp = remote(src, dst, sems.at[i, 2], sems.at[i, 3], "row")
            cp.start()
            loc = pltpu.make_async_copy(keep, dst, sems.at[i, 6])
            loc.start()
            pending += [cp, loc]
        for i, cp in firsts:
            cp.wait_recv()
            fw = remote(
                outs[i].at[1 - c, r], outs[i].at[1 - c, r], sems.at[i, 4], sems.at[i, 5], "row"
            )
            fw.start()
            pending.append(fw)
        for _, cp in firsts:
            cp.wait_send()
        for cp in pending:
            cp.wait()

    outs = []
    for kind, a in zip(kinds, arrays):
        if kind == "all":
            s = (2, 2) + a.shape
        elif kind == "row":
            s = (2,) + a.shape
        elif kind == "lead":
            s = a.shape
        else:
            s = (2, a.shape[0], a.shape[1] // 2)
        outs.append(jax.ShapeDtypeStruct(s, a.dtype))
    return call(body, outs, [pltpu.SemaphoreType.DMA((n, 7))], arrays, cid)


def scatter_scratch(part):
    s, d = part.shape[2:], part.dtype
    return [
        pltpu.VMEM((2,) + s, d),
        pltpu.VMEM(s, d),
        pltpu.VMEM(s, d),
        pltpu.SemaphoreType.DMA((6,)),
    ]


def scatter_sum(part, land, out_x, land_x, sems):
    r, c = lax.axis_index("row"), lax.axis_index("col")
    first = remote(part.at[1 - c, 1 - r], land.at[0], sems.at[0], sems.at[1], "row")
    second = remote(part.at[c, 1 - r], land.at[1], sems.at[2], sems.at[3], "row")
    first.start()
    second.start()
    first.wait_recv()
    out_x[...] = (part[1 - c, r].astype(F32) + land[0].astype(F32)).astype(out_x.dtype)
    third = remote(out_x, land_x, sems.at[4], sems.at[5], "col")
    third.start()
    second.wait_recv()
    mine = part[c, r].astype(F32) + land[1].astype(F32)
    third.wait_recv()
    total = mine + land_x[...].astype(F32)

    def finish():
        first.wait_send()
        second.wait_send()
        third.wait_send()

    return total, finish


def reduce_out(part, resid, cid):
    def body(part, resid, out, land, out_x, land_x, sems):
        greet(("row", "col"))
        total, finish = scatter_sum(part, land, out_x, land_x, sems)
        out[...] = (total + resid[...]).astype(BF16)
        finish()

    outs = [jax.ShapeDtypeStruct(resid.shape, BF16)]
    return call(body, outs, scatter_scratch(part), [part, resid], cid)[0]


def norm_back(grad, resid, gain):
    width = resid.shape[1]
    inv = lax.rsqrt(jnp.sum(resid * resid, axis=1, keepdims=True) / width + epsilon)
    unit = resid * inv
    weighted = grad * gain
    mean = jnp.sum(weighted * unit, axis=1, keepdims=True) / width
    return inv * (weighted - unit * mean), jnp.sum(grad * unit, axis=0, keepdims=True)


def mid_back(part, mid, og, gain, cid):
    def body(part, mid, og, gain, mg, mg_all, gg, land, out_x, land_x, sems, sems2):
        r, c = lax.axis_index("row"), lax.axis_index("col")
        greet(("row", "col"))
        total, finish = scatter_sum(part, land, out_x, land_x, sems)
        back, gsum = norm_back(total, mid[...], gain[...])
        back = back + og[...].astype(F32)
        mg_all[c, r] = back.astype(BF16)
        mine = mg_all.at[c, r]
        a = remote(mine, mine, sems2.at[0], sems2.at[1], "col")
        b = remote(mine, mine, sems2.at[2], sems2.at[3], "row")
        a.start()
        b.start()
        mg[...] = back
        gg[...] = gsum
        a.wait_recv()
        theirs = mg_all.at[1 - c, r]
        f = remote(theirs, theirs, sems2.at[4], sems2.at[5], "row")
        f.start()
        a.wait_send()
        b.wait()
        f.wait()
        finish()

    t, w = mid.shape
    outs = [
        jax.ShapeDtypeStruct((t, w), F32),
        jax.ShapeDtypeStruct((2, 2, t, w), BF16),
        jax.ShapeDtypeStruct((1, w), F32),
    ]
    scratch = scatter_scratch(part) + [pltpu.SemaphoreType.DMA((6,))]
    return call(body, outs, scratch, [part, mid, og, gain], cid)


def in_back(part, hid, mg, gain, cid):
    def body(part, hid, mg, gain, out, gg, land, out_x, land_x, sems, swap, got, sems2):
        r, c = lax.axis_index("row"), lax.axis_index("col")
        greet(("row", "col"))
        total, finish = scatter_sum(part, land, out_x, land_x, sems)
        back, gsum = norm_back(total, hid[...].astype(F32), gain[...])
        back = back + mg[...]
        w = back.shape[1] // 2
        swap[0] = back[:, :w]
        swap[1] = back[:, w:]
        a = remote(swap.at[1 - r], got, sems2.at[0], sems2.at[1], "row")
        a.start()
        gg[...] = gsum
        out[r] = swap[r]
        a.wait()
        out[1 - r] = got[...]
        finish()

    t, w = hid.shape
    outs = [jax.ShapeDtypeStruct((2, t, w // 2), F32), jax.ShapeDtypeStruct((1, w), F32)]
    scratch = scatter_scratch(part) + [
        pltpu.VMEM((2, t, w // 2), F32),
        pltpu.VMEM((t, w // 2), F32),
        pltpu.SemaphoreType.DMA((2,)),
    ]
    return call(body, outs, scratch, [part, hid, mg, gain], cid)


def head(values, h):
    return values[:, h * HEAD_SIZE : (h + 1) * HEAD_SIZE]


def turn(x, xp, cos, sin):
    x, xp = x.astype(F32), xp.astype(F32)
    return (x * cos + xp * sin).astype(BF16), (xp * cos - x * sin).astype(BF16)


def pick(flag, a, b):
    return jnp.where(flag, b, a)


def attn_forward(q, k, v, qp, kp, cos, sin, seg_col, seg_row, sel):
    heads = q.shape[1] // HEAD_SIZE
    t = q.shape[0]

    def body(sel, q, k, v, qp, kp, cos, sin, seg_c, seg_r, out, lt, qr, qrp, kr, krp):
        co, si = cos[...], sin[...]
        at = lax.broadcasted_iota(jnp.int32, (t, t), 0)
        to = lax.broadcasted_iota(jnp.int32, (t, t), 1)
        allowed = (seg_c[...] == seg_r[...]) & (to <= at)
        kk = []
        for g in range(2):
            a, b = turn(head(k, g), head(kp, g), co, si)
            kr[:, g * HEAD_SIZE : (g + 1) * HEAD_SIZE] = a
            krp[:, g * HEAD_SIZE : (g + 1) * HEAD_SIZE] = b
            kk.append(a)
        vv = [head(v, 0), head(v, 1)]
        for h in range(heads):
            a, b = turn(head(q, h), head(qp, h), co, si)
            qr[:, h * HEAD_SIZE : (h + 1) * HEAD_SIZE] = a
            qrp[:, h * HEAD_SIZE : (h + 1) * HEAD_SIZE] = b
            f = sel[h] == 1
            s = contract_cols(a, pick(f, *kk)) * HEAD_SIZE**-0.5
            s = jnp.where(allowed, s, masked_score)
            m = jnp.max(s, axis=1, keepdims=True)
            l = m + jnp.log(jnp.sum(jnp.exp(s - m), axis=1, keepdims=True))
            lt[:, h : h + 1] = l
            p = jnp.exp(s - l).astype(BF16)
            out[:, h * HEAD_SIZE : (h + 1) * HEAD_SIZE] = matmul(p, pick(f, *vv)).astype(BF16)

    outs = [
        jax.ShapeDtypeStruct(q.shape, BF16),
        jax.ShapeDtypeStruct((t, heads), F32),
        jax.ShapeDtypeStruct(q.shape, BF16),
        jax.ShapeDtypeStruct(q.shape, BF16),
        jax.ShapeDtypeStruct(k.shape, BF16),
        jax.ShapeDtypeStruct(k.shape, BF16),
    ]
    return pl.pallas_call(
        body,
        out_shape=outs,
        in_specs=[pl.BlockSpec(memory_space=pltpu.SMEM)] + [VM] * 9,
        out_specs=[VM] * 6,
        compiler_params=pltpu.CompilerParams(vmem_limit_bytes=60 * 2**20),
        name="attn_forward",
    )(sel, q, k, v, qp, kp, cos, sin, seg_col, seg_row)


def attn_backward(qr, qrp, kr, krp, v, lt, att, da, cos, sin, seg_col, seg_row, sel):
    heads = qr.shape[1] // HEAD_SIZE
    t = qr.shape[0]
    kw = kr.shape[1]

    def body(sel, qr, qrp, kr, krp, v, lt, att, da, cos, sin, seg_c, seg_r, out):
        co, si = cos[...], sin[...]
        at = lax.broadcasted_iota(jnp.int32, (t, t), 0)
        to = lax.broadcasted_iota(jnp.int32, (t, t), 1)
        allowed = (seg_c[...] == seg_r[...]) & (to <= at)
        kk = [jnp.concatenate([head(kr, g), head(krp, g)], axis=1) for g in range(2)]
        vv = [head(v, 0), head(v, 1)]
        dk = [jnp.zeros((t, 2 * HEAD_SIZE), F32)] * 2
        dv = [jnp.zeros((t, HEAD_SIZE), F32)] * 2
        for h in range(heads):
            f = sel[h] == 1
            kc = pick(f, *kk)
            vh = pick(f, *vv)
            qh = head(qr, h)
            dh = head(da, h)
            s = contract_cols(qh, kc[:, :HEAD_SIZE]) * HEAD_SIZE**-0.5
            s = jnp.where(allowed, s, masked_score)
            p = jnp.exp(s - lt[:, h : h + 1])
            dot = jnp.sum(dh.astype(F32) * head(att, h).astype(F32), axis=1, keepdims=True)
            dvh = contract_rows(p.astype(BF16), dh)
            dp = contract_cols(dh, vh)
            ds = (p * (dp - dot) * HEAD_SIZE**-0.5).astype(BF16)
            dq = matmul(ds, kc)
            dq = dq[:, :HEAD_SIZE] * co - dq[:, HEAD_SIZE:] * si
            out[:, h * HEAD_SIZE : (h + 1) * HEAD_SIZE] = dq.astype(BF16)
            dkh = contract_rows(ds, jnp.concatenate([qh, head(qrp, h)], axis=1))
            zk, zv = jnp.zeros_like(dkh), jnp.zeros_like(dvh)
            dk = [dk[0] + pick(f, dkh, zk), dk[1] + pick(f, zk, dkh)]
            dv = [dv[0] + pick(f, dvh, zv), dv[1] + pick(f, zv, dvh)]
        base = heads * HEAD_SIZE
        for g in range(2):
            lo = base + g * HEAD_SIZE
            back = dk[g][:, :HEAD_SIZE] * co - dk[g][:, HEAD_SIZE:] * si
            out[:, lo : lo + HEAD_SIZE] = back.astype(BF16)
            out[:, lo + kw : lo + kw + HEAD_SIZE] = dv[g].astype(BF16)

    return pl.pallas_call(
        body,
        out_shape=jax.ShapeDtypeStruct((t, heads * HEAD_SIZE + 2 * kw), BF16),
        in_specs=[pl.BlockSpec(memory_space=pltpu.SMEM)] + [VM] * 12,
        out_specs=VM,
        compiler_params=pltpu.CompilerParams(vmem_limit_bytes=60 * 2**20),
        name="attn_backward",
    )(sel, qr, qrp, kr, krp, v, lt, att, da, cos, sin, seg_col, seg_row)


def swap_halves(weights):
    w = weights.reshape(weights.shape[0], -1, 2, HEAD_SIZE // 2)
    return jnp.concatenate([-w[:, :, 1:], w[:, :, :1]], axis=2).reshape(weights.shape)


def flat(slots):
    a, b, t, w = slots.shape
    return jnp.transpose(slots, (0, 2, 1, 3)).reshape(a * t, b * w)


def ordered(r, mine, theirs, axis):
    return jnp.where(
        r == 0,
        jnp.concatenate([mine, theirs], axis=axis),
        jnp.concatenate([theirs, mine], axis=axis),
    )


PAIR = [(0, 1), (1, 0)]


def on_device(
    hidden_in,
    segment_ids,
    position_ids,
    attn_gain,
    query_weight,
    key_weight,
    value_matrix,
    output_weight,
    ffn_gain,
    gate_weight,
    up_weight,
    down_weight,
    out_grad,
):
    r, c = lax.axis_index("row"), lax.axis_index("col")
    t = segment_ids.shape[0]
    width = 2 * hidden_in.shape[1]
    qc, kc = query_weight.shape[1], key_weight.shape[1]
    half = qc % HEAD_SIZE
    fw = gate_weight.shape[1] // 2
    slots_q = (qc + half) // 2
    slots_k = 2 * HEAD_SIZE

    def edge_of(w):
        n = w.shape[1]
        return jnp.where(c == 0, w[:, n - half :], w[:, :half])

    own = jnp.concatenate([query_weight, key_weight, value_matrix], axis=1)
    edge = jnp.concatenate(
        [edge_of(query_weight), edge_of(key_weight), edge_of(value_matrix)], axis=1
    )
    gains = jnp.stack([attn_gain, ffn_gain])
    h_s, edge_s, gain_s, own_s, gate_s, up_s, down_s = exchange(
        ("all", "all", "row", "row", "cols", "cols", "lead"),
        [
            hidden_in,
            edge,
            gains,
            own,
            gate_weight,
            up_weight,
            down_weight.reshape(2, fw, down_weight.shape[1]),
        ],
        1,
    )
    output_weight, out_grad, h_s = lax.optimization_barrier((output_weight, out_grad, h_s))
    wo_x = lax.ppermute(output_weight, "col", PAIR)
    og_x = lax.ppermute(out_grad, "col", PAIR)
    gains = jnp.transpose(gain_s, (1, 0, 2)).reshape(2, width)
    g_one, g_two = gains[0:1], gains[1:2]
    hid = flat(h_s)
    resid = hid.astype(F32)

    frequency = rope_base ** (
        -(jnp.arange(HEAD_SIZE // 2, dtype=F32) * 2.0) / HEAD_SIZE
    )
    angles = position_ids.astype(F32)[:, None] * frequency[None, :]
    cos, sin = jnp.cos(angles), jnp.sin(angles)
    cos = jnp.concatenate([cos, cos], axis=1)
    sin = jnp.concatenate([sin, sin], axis=1)

    own = own_s.reshape(width, qc + 2 * kc)
    edge_x = lax.dynamic_index_in_dim(edge_s, 1 - c, 0, keepdims=False).reshape(width, 3 * half)

    def local(lo, n, e, size):
        ext = ordered(c, own[:, lo : lo + n], edge_x[:, e * half : (e + 1) * half], 1)
        step = (ext.shape[1] - size)
        return lax.dynamic_slice_in_dim(ext, r * step, size, 1)

    wq = local(0, qc, 0, slots_q)
    wk = local(qc, kc, 1, slots_k)
    wv = local(qc + kc, kc, 2, slots_k)
    w_three = jnp.concatenate([wq, wk, wv], axis=1)
    w_all = jnp.concatenate([w_three, swap_halves(wq), swap_halves(wk)], axis=1)
    inv_one = lax.rsqrt(jnp.mean(resid * resid, axis=1, keepdims=True) + epsilon)
    normed_one = (resid * inv_one * g_one).astype(BF16)
    proj = matmul(normed_one, w_all).astype(BF16)
    e1, e2, e3, e4 = slots_q, slots_q + slots_k, slots_q + 2 * slots_k, 2 * slots_q + 2 * slots_k
    q, k, v, qp, kp = proj[:, :e1], proj[:, e1:e2], proj[:, e2:e3], proj[:, e3:e4], proj[:, e4:]
    heads = slots_q // HEAD_SIZE
    group = QUERY_HEADS // KEY_VALUE_HEADS
    first = c * (QUERY_HEADS - 2 * heads) + r * heads
    sel = (first + jnp.arange(heads, dtype=jnp.int32)) // group - first // group
    seg_col, seg_row = segment_ids[:, None], segment_ids[None, :]
    att, lt, qr, qrp, kr, krp = attn_forward(q, k, v, qp, kp, cos, sin, seg_col, seg_row, sel)

    pair_wo = jnp.stack([output_weight, wo_x])
    pair_og = jnp.stack([out_grad, og_x])
    att_s, wo_s, og_s = exchange(("all", "row", "row"), [att, pair_wo, pair_og], 2)
    def cols_first(s):
        s = jnp.where(c == 0, s, s[:, ::-1])
        return jnp.transpose(s, (1, 0, 2, 3))

    wo = flat(cols_first(wo_s))
    og = flat(cols_first(og_s))
    att_all = jnp.transpose(att_s.reshape(4, t, slots_q), (1, 0, 2)).reshape(t, 4 * slots_q)
    wo_pad = jnp.concatenate(
        [wo[: 2 * slots_q], jnp.zeros((HEAD_SIZE, width), BF16), wo[2 * slots_q :]], axis=0
    )
    mid = resid + matmul(att_all, wo_pad)
    inv_two = lax.rsqrt(jnp.mean(mid * mid, axis=1, keepdims=True) + epsilon)
    normed_two = (mid * inv_two * g_two).astype(BF16)
    gate_w = gate_s.reshape(width, fw)
    up_w = up_s.reshape(width, fw)
    gate = matmul(normed_two, gate_w)
    up = matmul(normed_two, up_w)
    sig = jax.nn.sigmoid(gate)
    silu = gate * sig
    inner = (silu * up).astype(BF16)
    down_w = jnp.transpose(down_s, (1, 0, 2)).reshape(fw, width)
    inner_grad = contract_cols(og, down_w)
    gate_grad = (inner_grad * up * sig * (1.0 + gate * (1.0 - sig))).astype(BF16)
    up_grad = (inner_grad * silu).astype(BF16)
    both = jnp.concatenate([gate_grad, up_grad], axis=1)
    both_w = jnp.concatenate([gate_w, up_w], axis=1)
    part_two = contract_cols(both, both_w).astype(BF16).reshape(2, 2, t // 4, width)

    slot = 2 * c + r
    def quarter(x):
        return lax.dynamic_slice_in_dim(x, slot * (t // 4), t // 4, 0)

    mg, mg_s, gg_two = mid_back(part_two, quarter(mid), quarter(og), g_two, 3)
    mg_all = mg_s.reshape(t, width)
    wo_mine = lax.dynamic_slice_in_dim(wo_pad, slot * slots_q, slots_q, 0)
    da = contract_cols(mg_all, wo_mine).astype(BF16)
    pg = attn_backward(qr, qrp, kr, krp, v, lt, att, da, cos, sin, seg_col, seg_row, sel)
    part_one = contract_cols(pg, w_three).astype(BF16).reshape(2, 2, t // 4, width)
    in_grad, gg_one = in_back(part_one, quarter(hid), mg, g_one, 4)
    hidden_in_grad = in_grad.reshape(t // 2, width // 2)

    def row_half(x):
        return lax.dynamic_slice_in_dim(x, r * (width // 2), width // 2, 1)

    hand = jnp.concatenate([both, inner], axis=1)
    hand_x = lax.ppermute(hand, "row", PAIR)
    gate_full = ordered(r, hand[:, :fw], hand_x[:, :fw], 1)
    up_full = ordered(r, hand[:, fw : 2 * fw], hand_x[:, fw : 2 * fw], 1)
    inner_full = ordered(r, hand[:, 2 * fw :], hand_x[:, 2 * fw :], 1)
    n2 = row_half(normed_two)
    gate_wg = contract_rows(n2, gate_full).astype(BF16)
    up_wg = contract_rows(n2, up_full).astype(BF16)
    down_wg = contract_rows(inner_full, row_half(og)).astype(BF16)
    down_t = lax.psum_scatter(down_wg[None], "dp", scatter_dimension=1, tiled=True).astype(F32)
    gate_t = lax.psum_scatter(gate_wg[None], "dp", scatter_dimension=2, tiled=True).astype(F32)
    up_t = lax.psum_scatter(up_wg[None], "dp", scatter_dimension=2, tiled=True).astype(F32)

    part_out = jnp.stack(
        [matmul(inner, down_s[0]).astype(BF16), matmul(inner, down_s[1]).astype(BF16)]
    ).reshape(2, 2, t // 2, width // 2)
    part_out = jnp.transpose(part_out, (1, 0, 2, 3))
    my_mid = lax.dynamic_slice(mid, (c * (t // 2), r * (width // 2)), (t // 2, width // 2))
    hidden_out = reduce_out(part_out, my_mid, 5)

    att15 = jnp.concatenate(
        [att_all[:, : 2 * slots_q], att_all[:, 2 * slots_q + HEAD_SIZE :]], axis=1
    )
    att_c = lax.dynamic_slice_in_dim(att15, c * qc, qc, 1)
    out_wg = contract_rows(att_c, row_half(mg_all))
    pg_x = lax.ppermute(pg, "row", PAIR)
    pg0 = jnp.where(r == 0, pg, pg_x).astype(F32)
    pg1 = jnp.where(r == 0, pg_x, pg).astype(F32)
    ext_q = jnp.concatenate([pg0[:, :e1], pg1[:, :e1]], axis=1)

    def ext_of(lo):
        z = jnp.zeros((t, HEAD_SIZE), F32)
        a, b = pg0[:, lo : lo + slots_k], pg1[:, lo : lo + slots_k]
        return jnp.concatenate([a, z], axis=1) + jnp.concatenate([z, b], axis=1)

    exts = [ext_q, ext_of(e1), ext_of(e2)]
    sends = [jnp.where(c == 0, x[:, -half:], x[:, :half]) for x in exts]
    got = lax.ppermute(jnp.concatenate(sends, axis=1).astype(BF16), "col", PAIR).astype(F32)
    finals = []
    for i, x in enumerate(exts):
        n = x.shape[1]
        g = got[:, i * half : (i + 1) * half]
        low = jnp.concatenate([x[:, : n - 2 * half], x[:, n - 2 * half : n - half] + g], axis=1)
        high = jnp.concatenate([x[:, half : 2 * half] + g, x[:, 2 * half :]], axis=1)
        finals.append(jnp.where(c == 0, low, high).astype(BF16))
    proj_wg = contract_rows(row_half(normed_one), jnp.concatenate(finals, axis=1))
    proj_t, out_t = lax.psum((proj_wg.astype(BF16), out_wg.astype(BF16)), "dp")
    gain_t = lax.psum(jnp.concatenate([gg_one, gg_two], axis=0), ("dp", "row", "col"))
    gain_t = row_half(gain_t)
    proj_t = proj_t.astype(F32)
    return (
        hidden_out,
        hidden_in_grad,
        gain_t[0],
        proj_t[:, :qc],
        proj_t[:, qc : qc + kc],
        proj_t[:, qc + kc :],
        out_t.astype(F32),
        gain_t[1],
        gate_t,
        up_t,
        down_t,
    )


def solution(mesh):
    return jax.shard_map(
        on_device,
        mesh=mesh,
        in_specs=(
            P(("dp", "col"), "row"),
            P("dp"),
            P("dp"),
            P("row"),
            P("row", "col"),
            P("row", "col"),
            P("row", "col"),
            P("col", "row"),
            P("row"),
            P("row", "col"),
            P("row", "col"),
            P("col", "row"),
            P(("dp", "col"), "row"),
        ),
        out_specs=(
            P(("dp", "col"), "row"),
            P(("dp", "col"), "row"),
            P("row"),
            P("row", "col"),
            P("row", "col"),
            P("row", "col"),
            P("col", "row"),
            P("row"),
            P("col", "row", "dp"),
            P("col", "row", "dp"),
            P("col", "dp", "row"),
        ),
        check_vma=False,
    )
```

time: 678 us -> 475 us (0.70); the launches traced: 676 us -> 466 us
  waiting for transfers between devices: 416 us -> 169 us
  Pallas kernels: 0 us -> 95.3 us
  blocking collectives: 125 us -> 40.5 us
  local copies, waits for them, and re-layouts: 44.9 us -> 85.3 us
  matrix products: 45.8 us -> 26.6 us
    psum x1, waiting for transfers between devices: 304 us -> 0.01 us  [on_device(): proj_t, out_t = lax.psum((proj_wg.astype(BF16), out_wg.astype(BF16)), 'dp')]
    unnamed x13 -> x7, waiting for transfers between devices: 0.73 us -> 164 us
    pallas_call x0 -> x7, Pallas kernels: none -> 95.3 us  [the longest x5 79.9 us: call(): pl.pallas_call(body, out_shape=outs, in_specs=[VM] * len(args), out_specs...]
    reduce_scatter x10 -> x0, waiting for transfers between devices: 90.6 us -> none  [the longest x4 31.5 us: sum_over_rows(): lax.psum_scatter(partial_value, 'row', scatter_dimension=0, tiled=True)]
    all_gather x8 -> x0, blocking collectives: 62.3 us -> none  [the longest x4 36.6 us: gather_over_cols(): return lax.all_gather(values, 'col', axis=0, tiled=True)]
    unnamed x85 -> x120, local copies, waits for them, and re-layouts: 18.3 us -> 48 us
    all_to_all x3 -> x0, blocking collectives: 25.6 us -> none  [the longest x2 17.3 us: from_heads(): lax.all_to_all(values, 'col', split_axis=1, concat_axis=0, tiled=True)]
    dot_general x14 -> x10, matrix products: 36.9 us -> 13.2 us  [the longest x4 6.81 us: contract_cols(): lax.dot_general(left, right, (((1,), (1,)), ((), ())), preferred_element_...]
  transfers between devices with their start and end apart: 14 -> 9, of which waited for: 10 -> 4; matrix products, arithmetic and copies ran while one was open for 10% -> 19% of each run, Pallas kernels for 0% -> 7%
where the time goes in v1:
time: 475 us; the launch traced here: 466 us
  waiting for transfers between devices  169 us (36%)
  Pallas kernels  95.3 us (20%)
  local copies, waits for them, and re-layouts  85.3 us (18%)
  blocking collectives  40.5 us (9%)
  other arithmetic  30.5 us (6%)
  matrix products  26.6 us (6%)
  between operations  15.1 us (3%)
    unnamed x7, waiting for transfers between devices  164 us
    pallas_call x5, Pallas kernels, call(): pl.pallas_call(body, out_shape=outs, in_specs=[VM] * len(args), out_specs...  79.9 us
    unnamed x120, local copies, waits for them, and re-layouts  48 us
    psum x1, blocking collectives, on_device(): lax.psum(jnp.concatenate([gg_one, gg_two], axis=0), ('dp', 'row', 'col'))  40.5 us
    dot_general x5, matrix products, contract_rows(): lax.dot_general(left, right, (((0,), (0,)), ((), ())), preferred_element_...  13.4 us
  transfers between devices with their start and end apart: 9, of which 4 were waited for; matrix products, arithmetic and copies ran while one was open for 19% of the time, Pallas kernels for 7%

profile of v1, /device:TPU:0, one launch (start us, length us, event | category | flops | bytes accessed | tf_op | source)
XLA Modules:
  0.0 466.2 jit_solution(1887636442354337210)
XLA Ops:
  7.2 1.1 copy.116
  9.5 1.1 copy.118
  10.7 1.1 pad_maximum_fusion.8.refs_3_
  12.6 1.5 copy.122
  15.5 19.5 %shard_map.212 = (bf16[2,2,256,480]{3,2,1,0:T(8,128)(2,1)}, bf16[2,2,480,96]{3,2,1,0:T(8,128)(2,1)}, f32[2,2,480]{2,1,0:T(2,128)}, bf16[2,480,800]{2,1,0:T(8,128...) custom-call(bf16[256,480]{1,0:T(8,128)(2,1)} %copy.123.refs_0_, ...), custom_call_target="tpu_custom_call" | custom-call | tf_op jit(solution)/shard_map/pallas_call | solution.py:54
  37.9 1.4 slice.273
  45.8 1.9 copy.166
  49.8 1.4 constant_dynamic-update-slice_fusion.4
  53.4 1.3 convolution_convert_fusion.4
  57.6 2.0 copy.139
  60.4 7.7 %attn_forward.1 = (bf16[512,256]{1,0:T(8,128)(2,1)}, f32[512,4]{1,0:T(8,128)}, bf16[512,256]{1,0:T(8,128)(2,1)}, bf16[512,256]{1,0:T(8,128)(2,1)}, bf16[512,128]{1,0:T(8,128)(2,1)}, /*index=5*/bf16[512,128]{1,0:T(8,128)(2,1)}) custom-call(s32[4]{0:T(128)} %fusion.96.sel, bf16[512,256]{1,0:T(8,128)(2,1)} %get-tuple-element.131.q, ...), custom_call_target="tpu_custom_call" | custom-call | tf_op jit(solution)/shard_map/attn_forward/pallas_call | solution.py:287
  68.1 1.9 pad_maximum_fusion.10.refs_2_
  70.0 2.2 pad_maximum_fusion.7.refs_1_
  72.2 12.8 %shard_map.213 = (bf16[2,2,512,256]{3,2,1,0:T(8,128)(2,1)}, bf16[2,2,480,480]{3,2,1,0:T(8,128)(2,1)}, bf16[2,2,256,480]{3,2,1,0:T(8,128)(2,1)}) custom-call(bf16[512,256]{1,0:T(8,128)(2,1)} %get-tuple-element.40.refs_0_.att, bf16[2,480,480]{2,1,0:T(8,128)(2,1)} %pad_maximum_fusion.7.refs_1_, bf16[2,256,480]{2,1,0:T(8,128)(2,1)} %pad_maximum_fusion.10.refs_2_), custom_call_target="tpu_custom_call" | custom-call | tf_op jit(solution)/shard_map/pallas_call | solution.py:54
  85.0 2.7 fusion.9
  87.7 3.3 copy.134
  91.1 5.6 %reshape.133 = bf16[960,960]{1,0:T(8,128)(2,1)S(1)} reshape(bf16[2,480,2,480]{3,2,1,0:T(2,128)(2,1)} %copy.134) | data formatting | bytes 3686400 | tf_op jit(solution)/shard_map/reshape | solution.py:355
  97.7 1.1 slice.288
  98.8 1.5 copy.133
  100.3 1.8 fusion.34
  102.1 2.1 copy.138
  104.3 1.5 copy.172
  105.8 2.1 fusion.117
  108.8 3.0 pad_maximum_fusion
  111.8 1.5 multiply_reduce_fusion
  117.2 1.4 multiply_convert_fusion.2
  119.5 1.5 fusion.10
  121.0 1.6 copy.140
  122.5 21.5 %shard_map.215 = (f32[128,960]{1,0:T(8,128)}, bf16[2,2,128,960]{3,2,1,0:T(8,128)(2,1)}, f32[1,960]{1,0:T(1,128)}) custom-call(bf16[2,2,128,960]{3,2,1,0:T(8,128)(2,1)} %bitcast.99, f32[128,960]{1,0:T(8,128)} %constant_dynamic-slice_fusion.2.mid, bf16[128,960]{1,0:T(8,128)(2,1)} %copy.170.og, f32[1,960]{1,0:T(1,128)} %slice.229.gain), custom_call_target="tpu_custom_call" | custom-call | tf_op jit(solution)/shard_map/pallas_call | solution.py:54
  144.1 2.5 convolution_convert_fusion.9.da
  146.6 7.7 %attn_backward.1 = bf16[512,512]{1,0:T(8,128)(2,1)} custom-call(s32[4]{0:T(128)} %fusion.96.sel, bf16[512,256]{1,0:T(8,128)(2,1)} %get-tuple-element.48.qr, bf16[512,256]{1,0:T(8,128)(2,1)} %get-tuple-element.49.qrp, bf16[512,128]{1,0:T(8,128)(2,1)} %get-tuple-element.50.kr, bf16[512,128]{1,0:T(8,128)(2,1)} %get-tuple-element.51.krp, ...), custom_call_target="tpu_custom_call" | custom-call | tf_op jit(solution)/shard_map/attn_backward/pallas_call | solution.py:338
  154.9 1.5 pad_maximum_fusion.1
  156.4 1.6 convolution_convert_fusion.6
  158.1 1.2 select_convert_fusion
  160.0 1.1 collective-permute-start.3
  161.6 4.3 collective-permute-done.3
  167.9 1.8 convolution_convert_fusion.5
  170.1 1.3 fusion.107
  171.6 2.1 fusion
  173.7 5.8 %copy.153 = bf16[1,480,1280]{1,0,2:T(2,128)(2,1)S(1)} copy(bf16[1,480,1280]{2,1,0:T(8,128)(2,1)} %fusion) | data formatting | bytes 2457600
  179.5 1.5 copy.178
  181.0 4.0 fusion.1
  185.0 5.7 %copy.155 = bf16[1,480,1280]{1,0,2:T(2,128)(2,1)S(1)} copy(bf16[1,480,1280]{2,1,0:T(8,128)(2,1)} %fusion.1) | data formatting | bytes 2457600
  190.8 1.4 copy.177
  192.3 3.9 fusion.2
  196.1 5.7 %copy.157 = bf16[1,1280,480]{2,0,1:T(2,128)(2,1)S(1)} copy(bf16[1,1280,480]{1,2,0:T(8,128)(2,1)} %fusion.2) | data formatting | bytes 2457600
  201.9 1.5 copy.176
  204.1 1.7 constant_dynamic-slice_fusion.hid
  205.8 2.1 dynamic_slice.50.resid
  208.6 1.3 copy.143
  209.9 13.9 %shard_map.216 = (f32[2,128,480]{2,1,0:T(8,128)}, f32[1,960]{1,0:T(1,128)}) custom-call(bf16[2,2,128,960]{3,2,1,0:T(8,128)(2,1)} %bitcast.100, bf16[128,960]{1,0:T(8,128)(2,1)} %constant_dynamic-slice_fusion.hid, f32[128,960]{1,0:T(8,128)} %get-tuple-element.55.mg, f32[1,960]{1,0:T(1,128)} %slice.230.gain), custom_call_target="tpu_custom_call" | custom-call | tf_op jit(solution)/shard_map/pallas_call | solution.py:54
  223.8 2.0 copy.146
  227.5 1.1 maximum_bitcast_fusion.part
  228.6 12.3 %shard_map.214 = bf16[256,480]{1,0:T(8,128)(2,1)} custom-call(bf16[2,2,256,480]{3,2,1,0:T(8,128)(2,1)} %maximum_bitcast_fusion.part, f32[256,480]{1,0:T(8,128)} %dynamic_slice.50.resid), custom_call_target="tpu_custom_call" | custom-call | tf_op jit(solution)/shard_map/pallas_call | solution.py:54
  240.9 1.8 copy.145
  242.7 40.5 %psum.21 = f32[2,960]{1,0:T(2,128)S(1)} all-reduce(f32[2,960]{1,0:T(2,128)S(1)} %pad_maximum_fusion.16), channel_id=1, replica_groups=mesh['dp'=8,'row'=2,'col'=2] {'dp','row','col'}, use_global_device_ids=true, to_apply=%region_2.3 | all-reduce | flops 1920 | bytes 15360 | tf_op jit(solution)/shard_map/psum | solution.py:550
  283.9 2.2 convert_element_type.114
  286.2 1.3 copy.147
  288.4 33.7 %reduce-scatter.10.cloned.1.call-done = bf16[160,480]{1,0:T(8,128)(2,1)} async-done(((bf16[1280,480]{1,0:T(8,128)(2,1)}), bf16[160,480]{1,0:T(8,128)(2,1)}) %reduce-scatter.10.cloned.1.call-update) | async-done | bytes 153616
  322.1 1.1 reshape_bitcast_fusion.2
  324.3 65.3 %reduce-scatter.12.cloned.1.call-done = bf16[160,480]{1,0:T(8,128)(2,1)} async-done(((bf16[1280,480]{1,0:T(8,128)(2,1)}), bf16[160,480]{1,0:T(8,128)(2,1)}) %reduce-scatter.12.cloned.1.call-update) | async-done | bytes 153616
  389.6 1.1 reshape_bitcast_fusion.1
  391.7 65.3 %reduce-scatter.14.cloned.1.call-done = bf16[160,480]{1,0:T(8,128)(2,1)} async-done(((bf16[1280,480]{1,0:T(8,128)(2,1)}), bf16[160,480]{1,0:T(8,128)(2,1)}) %reduce-scatter.14.cloned.1.call-update) | async-done | bytes 153616
  457.0 1.1 reshape_bitcast_fusion
  (189 shorter events, 39.4 us)
Async XLA Ops:
  7.2 3.5 copy-start.16
  7.2 276.7 %all-reduce.7.cloned.1.call-start = ((), (), s32[]{:S(2)}) async-start(), calls=%async_computation.6 | async-start | bytes 2621440 | tf_op jit(solution)/shard_map/psum | solution.py:549
  7.2 4.5 copy-start.31
  9.4 3.2 copy-start.14
  11.8 2.3 copy-start.39
  11.8 2.3 copy-start.40
  15.5 19.5 %copy-start.32 = (bf16[256,480]{0,1:T(8,128)(2,1)S(1)}, bf16[256,480]{0,1:T(8,128)(2,1)}, u32[]{:S(2)}) copy-start(bf16[256,480]{0,1:T(8,128)(2,1)} %param.25) | copy-start | bytes 737284
  35.8 32.3 %collective-permute-start.1 = (bf16[256,480]{1,0:T(8,128)(2,1)}, bf16[256,480]{1,0:T(8,128)(2,1)}, u32[]{:S(2)}, u32[]{:S(2)}) collective-permute-start(bf16[256,480]{1,0:T(8,128)(2,1)} %copy.131), channel_id=1, source_target_pairs={{0,1},{1,0},{2,3},{3,2},{4,5},{5,4},{6,7},{7,6},{8,9},{9,8},{10,11... | collective-permute-start | bytes 737288 | tf_op jit(solution)/shard_map/ppermute | solution.py:417
  36.9 33.1 %collective-permute-start = (bf16[480,480]{1,0:T(8,128)(2,1)}, bf16[480,480]{1,0:T(8,128)(2,1)}, u32[]{:S(2)}, u32[]{:S(2)}) collective-permute-start(bf16[480,480]{1,0:T(8,128)(2,1)} %param.20), channel_id=1, source_target_pairs={{0,1},{1,0},{2,3},{3,2},{4,5},{5,4},{6,7},{7,6},{8,9},{9,8},{10,11... | collective-permute-start | bytes 1382408 | tf_op jit(solution)/shard_map/ppermute | solution.py:416
  37.9 1.8 copy-start.6
  37.9 2.8 copy-start.38
  39.6 3.7 copy-start.35
  39.6 3.7 copy-start.3
  40.6 3.1 copy-start.33
  49.8 62.1 %copy-start = (bf16[512,960]{1,0:T(8,128)(2,1)}, bf16[512,960]{1,0:T(8,128)(2,1)S(1)}, u32[]{:S(2)}) copy-start(bf16[512,960]{1,0:T(8,128)(2,1)S(1)} %reshape.148) | copy-start | bytes 2949124
  49.8 1.5 copy-start.11
  51.2 0.8 copy-start.7
  51.5 1.5 copy-start.22
  53.3 1.3 copy-start.17
  53.4 3.4 copy-start.34
  53.4 4.2 copy-start.12
  104.3 1.6 copy-start.15
  105.8 2.1 copy-start.10
  105.8 3.0 copy-start.2
  108.8 3.0 copy-start.4
  113.3 1.5 copy-start.1
  114.3 1.3 copy-start.42
  114.8 1.7 copy-start.19
  115.6 1.3 copy-start.41
  115.6 1.7 copy-start.43
  118.7 0.8 copy-start.27
  118.7 36.1 %copy-start.24 = (bf16[512,640]{1,0:T(8,128)(2,1)}, bf16[512,640]{1,0:T(8,128)(2,1)S(1)}, u32[]{:S(2)}) copy-start(bf16[512,640]{1,0:T(8,128)(2,1)S(1)} %get-tuple-element.115) | copy-start | bytes 1966084
  118.7 36.1 %copy-start.26 = (bf16[512,640]{1,0:T(8,128)(2,1)}, bf16[512,640]{1,0:T(8,128)(2,1)S(1)}, u32[]{:S(2)}) copy-start(bf16[512,640]{1,0:T(8,128)(2,1)S(1)} %get-tuple-element.114) | copy-start | bytes 1966084
  146.6 8.2 %copy-start.28 = (bf16[512,640]{1,0:T(8,128)(2,1)S(1)}, bf16[512,640]{1,0:T(8,128)(2,1)}, u32[]{:S(2)}) copy-start(bf16[512,640]{1,0:T(8,128)(2,1)} %copy-done.27) | copy-start | bytes 1966084
  154.4 3.7 collective-permute-start.2
  154.8 1.6 copy-start.21
  156.3 1.7 copy-start.9
  156.3 13.8 %collective-permute-start.4 = (bf16[512,1920]{1,0:T(8,128)(2,1)}, bf16[512,1920]{1,0:T(8,128)(2,1)S(1)}, u32[]{:S(2)}, u32[]{:S(2)}) collective-permute-start(bf16[512,1920]{1,0:T(8,128)(2,1)} %pad_maximum_fusion.1), channel_id=1, source_target_pairs={{0,2},{2,0},{1,3},{3,1},{4,6},{6,4},{5,7},{7,5},{8,10},{10,8},{9,1... | collective-permute-start | bytes 5898248 | tf_op jit(solution)/shard_map/ppermute | solution.py:504
  160.0 5.8 %collective-permute-start.3 = (bf16[512,96]{1,0:T(8,128)(2,1)S(1)}, bf16[512,96]{1,0:T(8,128)(2,1)S(1)}, u32[]{:S(2)}, u32[]{:S(2)}) collective-permute-start(bf16[512,96]{1,0:T(8,128)(2,1)S(1)} %pad_maximum_fusion.14), channel_id=1, source_target_pairs={{0,1},{1,0},{2,3},{3,2},{4,5},{5,4},{6,7},{7,6},{8,9},{9,8},{10,11... | collective-permute-start | bytes 294920 | tf_op jit(solution)/shard_map/ppermute | solution.py:540
  166.7 1.2 copy-start.18
  169.7 1.6 copy-start.29
  169.8 152.4 %reduce-scatter.10.cloned.1.call-start = ((), (), s32[]{:S(2)}) async-start(), calls=%async_computation.3 | async-start | bytes 1474560
  170.1 1.5 copy-start.20
  181.0 208.6 %reduce-scatter.12.cloned.1.call-start = ((), (), s32[]{:S(2)}) async-start(), calls=%async_computation.4 | async-start | bytes 1474560
  192.2 264.8 %reduce-scatter.14.cloned.1.call-start = ((), (), s32[]{:S(2)}) async-start(), calls=%async_computation.5 | async-start | bytes 1474560
  203.4 4.5 copy-start.8
  203.4 4.5 copy-start.23
  203.4 4.5 copy-start.30
  209.9 15.9 %copy-start.13 = (bf16[2,640,480]{2,1,0:T(8,128)(2,1)S(1)}, bf16[2,640,480]{2,1,0:T(8,128)(2,1)}, u32[]{:S(2)}) copy-start(bf16[2,640,480]{2,1,0:T(8,128)(2,1)} %get-tuple-element.47) | copy-start | bytes 3686404
  209.9 15.9 %copy-start.25 = (bf16[512,640]{1,0:T(8,128)(2,1)S(1)}, bf16[512,640]{1,0:T(8,128)(2,1)}, u32[]{:S(2)}) copy-start(bf16[512,640]{1,0:T(8,128)(2,1)} %copy-done.24) | copy-start | bytes 1966084
  227.5 15.2 %copy-start.36 = (f32[1,960]{1,0:T(1,128)S(1)}, f32[1,960]{1,0:T(1,128)}, u32[]{:S(2)}) copy-start(f32[1,960]{1,0:T(1,128)} %get-tuple-element.58) | copy-start | bytes 11524
  227.5 15.2 %copy-start.37 = (f32[1,960]{1,0:T(1,128)S(1)}, f32[1,960]{1,0:T(1,128)}, u32[]{:S(2)}) copy-start(f32[1,960]{1,0:T(1,128)} %get-tuple-element.57) | copy-start | bytes 11524
  283.9 2.2 copy-start.5
Sparse Core Ops, SparseCore 0:
  169.9 84.4 all-reduce.6
  257.8 64.3 reduce-scatter.9
  325.5 64.0 reduce-scatter.11
  392.8 64.1 reduce-scatter.13
